TPU v7x, 256 devices: a whole 4x4x8 slice. The times are simulated.
256 devices in a mesh: energy: 16 (over x, y), domain: 16 (over z, core).
Axes of the slice: x: 4, y: 4, z: 8, core: 2. Of those that a mesh axis runs over, the one named last changes fastest.
Arguments:
- retarded: bfloat16 [16, 32, 256, 512], P('energy', 'domain'), may hold values from -1 to 2
- coupling: bfloat16 [32, 256, 512], P('domain'), may hold values from -1 to 2
- sigma_lesser: bfloat16 [16, 32, 256, 512], P('energy', 'domain'), may hold values from -4 to 4
- sigma_greater: bfloat16 [16, 32, 256, 512], P('energy', 'domain'), may hold values from -4 to 4
- tiles: int32 [32, 2], P('domain'), may hold values from 0 to 3, all different within a row
- offsets: int32 [16], replicated, may hold values from -8 to 8, as said below
Outputs:
- polarization: bfloat16 [16, 32, 2, 128, 256], P('energy', 'domain')
Inputs may be any that keep to these rules, and one draw needn't show every extreme that they name: Each row names 2 different tiles. `offsets`: both ends of the range occur in every draw.
All inputs are finite; a program needn't handle non-finite values.
Results may differ from a plain program's by a relative error of at most 0.039.
Values may be sent and summed in bfloat16 or wider, within the bound.
A program may use at most 64 MiB of HBM per device.

v0:
```python
import jax
import jax.numpy as jnp
from jax import lax
from jax.sharding import PartitionSpec as P


def passed_along(block, axis, distance):
    devices = range(lax.axis_size(axis))
    route = [(i - distance, i) for i in devices if i - distance in devices]
    return lax.ppermute(block, axis, route)


def stacked(block):
    block_order = block.shape[-2]
    real_part = block[..., :block_order]
    imag_part = block[..., block_order:]
    bottom = jnp.concatenate([-imag_part, real_part], axis=-1)
    return jnp.concatenate([block, bottom], axis=-2)


def product(factor, second):
    return jnp.matmul(factor, stacked(second), preferred_element_type=jnp.float32)


def product_adjoint(factor, second):
    return jnp.matmul(
        factor, jnp.swapaxes(stacked(second), -1, -2), preferred_element_type=jnp.float32
    )


def advance(carried, propagator, injected):
    moved = product(propagator[None], carried).astype(jnp.bfloat16)
    return (product_adjoint(moved, propagator[None]) + injected.astype(jnp.float32)).astype(
        jnp.bfloat16
    )


def to_tiles(block, tile_rows):
    leading = block.shape[:-2]
    leading_count = len(leading)
    pieces = block.reshape(leading + (2, tile_rows, 2, 2, tile_rows))
    axes_order = tuple(range(leading_count)) + (
        leading_count,
        leading_count + 3,
        leading_count + 1,
        leading_count + 2,
        leading_count + 4,
    )
    return pieces.transpose(axes_order).reshape(leading + (4, tile_rows, 2 * tile_rows))


def convolve(less_tiles, great_tiles, offsets):
    energies = less_tiles.shape[0]
    tile_rows = less_tiles.shape[-1] // 2
    pad_shape = (energies,) + great_tiles.shape[1:]
    padding = jnp.zeros(pad_shape, great_tiles.dtype)
    padded = jnp.concatenate([padding, great_tiles, padding], axis=0)

    def one_output(offset):
        begin_at = energies - offset
        shifted = lax.dynamic_slice_in_dim(padded, begin_at, energies, 0).astype(jnp.float32)
        less_real = less_tiles[..., :tile_rows].astype(jnp.float32)
        less_imag = less_tiles[..., tile_rows:].astype(jnp.float32)
        great_real = shifted[..., :tile_rows]
        great_imag = shifted[..., tile_rows:]
        out_real = jnp.sum(less_real * great_real - less_imag * great_imag, axis=0)
        out_imag = jnp.sum(less_real * great_imag + less_imag * great_real, axis=0)
        return (jnp.concatenate([out_real, out_imag], axis=-1) / energies).astype(jnp.bfloat16)

    return lax.map(one_output, offsets)


def pick_tiles(all_tiles, selector):
    return jnp.einsum(
        "ksz,ekzrc->eksrc", selector, all_tiles, preferred_element_type=jnp.float32
    ).astype(jnp.bfloat16)


def shards(retarded, coupling, sigma_lesser, sigma_greater, tiles, offsets):
    block_order = retarded.shape[2]
    tile_rows = block_order // 2
    blocks = retarded.shape[1]
    propagator = product(retarded, coupling[None]).astype(jnp.bfloat16)
    sigmas = jnp.stack([sigma_lesser, sigma_greater])
    injected = product_adjoint(
        product(retarded[None], sigmas).astype(jnp.bfloat16), retarded[None]
    ).astype(jnp.bfloat16)
    composite = propagator[:, 0]
    carried = injected[:, :, 0]
    position = 1
    carried = advance(carried, propagator[:, position], injected[:, :, position])
    composite = product(propagator[:, position], composite).astype(jnp.bfloat16)

    def relay_turn(turn, arrived):
        outgoing = advance(arrived, composite, carried)
        return passed_along(outgoing, "domain", 1)

    incoming = lax.fori_loop(0, lax.axis_size("domain") - 1, relay_turn, jnp.zeros_like(carried))
    current = incoming
    collected = []
    for position in range(blocks):
        current = advance(current, propagator[:, position], injected[:, :, position])
        collected.append(current)
    swept = jnp.stack(collected, axis=2)
    all_tiles = to_tiles(swept, tile_rows)
    selector = (tiles[:, :, None] == jnp.arange(4, dtype=jnp.int32)[None, None, :]).astype(
        jnp.bfloat16
    )
    chosen_less = pick_tiles(all_tiles[0], selector)
    chosen_great = pick_tiles(all_tiles[1], selector)
    less_part = lax.all_to_all(chosen_less, "energy", split_axis=3, concat_axis=0, tiled=True)
    great_part = lax.all_to_all(chosen_great, "energy", split_axis=3, concat_axis=0, tiled=True)
    result = convolve(less_part, great_part, offsets)
    return lax.all_to_all(result, "energy", split_axis=0, concat_axis=3, tiled=True)


def solution(mesh):
    placed = (
        P("energy", "domain", None, None),
        P("domain", None, None),
        P("energy", "domain", None, None),
        P("energy", "domain", None, None),
        P("domain", None),
        P(),
    )
    return jax.shard_map(
        shards,
        mesh=mesh,
        in_specs=placed,
        out_specs=P("energy", "domain", None, None, None),
        check_vma=False,
    )
```

profile of v0, /device:TPU:128, one launch (start us, length us, event | category | flops | bytes accessed | tf_op | source)
XLA Modules:
  0.0 312.0 jit_solution(11728612346050206011)
XLA Ops:
  0.0 1.3 copy.15
  2.0 0.8 fusion.113
  2.9 0.8 slice_negate_fusion.6
  4.4 0.8 slice_negate_fusion.3
  5.4 3.3 %fusion.33 = bf16[2,1,2,256,512]{4,3,0,2,1:T(8,128)(2,1)} fusion(bf16[1,1,2,256,256]{3,4,2,1,0:T(8,128)(2,1)} %get-tuple-element.178, bf16[1,1,2,256,256]{3,4,2,1,0:T(8,128)(2,1)} %get-tuple-element.177, bf16[1,1,2,256,512]{3,4,2,1,0:T(8,128)(2,1)S(1)} %bitcast.213, bf16[1,2,256,512]{3,2,1,0:T(8,128)(2,1)S(1)} %copy-done.2, ...), kind=kOutput, calls=%fused_computation.35 | convolution fusion | flops 1088421888 | bytes 4194304 | tf_op jit(solution)/shard_map/dot_general | solution.py:26
  8.7 1.2 slice_bitcast_fusion.1
  10.2 1.5 fusion.38
  11.8 217.7 %while.24 = (s32[]{:T(128)}, bf16[2,1,256,512]{3,2,0,1:T(8,128)(2,1)S(1)}, bf16[1,256,512]{2,1,0:T(8,128)(2,1)S(1)}, bf16[1,1,512,512]{2,3,1,0:T(8,128)(2,1)S(1)}, bf16[2,1,256,512]{3,2,0,1:T(8,128)(2,1)}, /*index=5*/s32[]{:T(128)}) while((s32[]{:T(128)}, bf16[2,1,256,512]{3,2,0,1:T(8,128)(2,1)S(1)}, bf16[1,256,512]{2,1,0:T(8,128)(2,1)S(1)}, ...), condition=%wide.region_1.0_spmd, body=%wide.region_0.0_spmd.sunk | while | flops 541196288 | bytes 6029421 | solution.py:98
  11.8 2.6 fusion.127
  14.4 1.9 collective-permute-start
  16.3 10.0 %collective-permute-done = bf16[2,1,256,512]{3,2,0,1:T(8,128)(2,1)S(1)} collective-permute-done((bf16[2,1,256,512]{3,2,0,1:T(8,128)(2,1)}, bf16[2,1,256,512]{3,2,0,1:T(8,128)(2,1)S(1)}, u32[]{:S(2)}, u32[]{:S(2)}) %collective-permute-start) | collective-permute-done | bytes 524320 | tf_op jit(solution)/shard_map/while/body/eval_jaxpr/ppermute | solution.py:10
  26.3 2.6 fusion.127
  28.9 1.9 collective-permute-start
  30.8 10.0 %collective-permute-done = bf16[2,1,256,512]{3,2,0,1:T(8,128)(2,1)S(1)} collective-permute-done((bf16[2,1,256,512]{3,2,0,1:T(8,128)(2,1)}, bf16[2,1,256,512]{3,2,0,1:T(8,128)(2,1)S(1)}, u32[]{:S(2)}, u32[]{:S(2)}) %collective-permute-start) | collective-permute-done | bytes 524320 | tf_op jit(solution)/shard_map/while/body/eval_jaxpr/ppermute | solution.py:10
  40.9 2.6 fusion.127
  43.4 1.9 collective-permute-start
  45.3 10.0 %collective-permute-done = bf16[2,1,256,512]{3,2,0,1:T(8,128)(2,1)S(1)} collective-permute-done((bf16[2,1,256,512]{3,2,0,1:T(8,128)(2,1)}, bf16[2,1,256,512]{3,2,0,1:T(8,128)(2,1)S(1)}, u32[]{:S(2)}, u32[]{:S(2)}) %collective-permute-start) | collective-permute-done | bytes 524320 | tf_op jit(solution)/shard_map/while/body/eval_jaxpr/ppermute | solution.py:10
  55.4 2.6 fusion.127
  57.9 1.9 collective-permute-start
  59.9 10.0 %collective-permute-done = bf16[2,1,256,512]{3,2,0,1:T(8,128)(2,1)S(1)} collective-permute-done((bf16[2,1,256,512]{3,2,0,1:T(8,128)(2,1)}, bf16[2,1,256,512]{3,2,0,1:T(8,128)(2,1)S(1)}, u32[]{:S(2)}, u32[]{:S(2)}) %collective-permute-start) | collective-permute-done | bytes 524320 | tf_op jit(solution)/shard_map/while/body/eval_jaxpr/ppermute | solution.py:10
  69.9 2.6 fusion.127
  72.4 1.9 collective-permute-start
  74.4 10.0 %collective-permute-done = bf16[2,1,256,512]{3,2,0,1:T(8,128)(2,1)S(1)} collective-permute-done((bf16[2,1,256,512]{3,2,0,1:T(8,128)(2,1)}, bf16[2,1,256,512]{3,2,0,1:T(8,128)(2,1)S(1)}, u32[]{:S(2)}, u32[]{:S(2)}) %collective-permute-start) | collective-permute-done | bytes 524320 | tf_op jit(solution)/shard_map/while/body/eval_jaxpr/ppermute | solution.py:10
  84.4 2.6 fusion.127
  87.0 1.9 collective-permute-start
  88.9 10.0 %collective-permute-done = bf16[2,1,256,512]{3,2,0,1:T(8,128)(2,1)S(1)} collective-permute-done((bf16[2,1,256,512]{3,2,0,1:T(8,128)(2,1)}, bf16[2,1,256,512]{3,2,0,1:T(8,128)(2,1)S(1)}, u32[]{:S(2)}, u32[]{:S(2)}) %collective-permute-start) | collective-permute-done | bytes 524320 | tf_op jit(solution)/shard_map/while/body/eval_jaxpr/ppermute | solution.py:10
  98.9 2.6 fusion.127
  101.5 1.9 collective-permute-start
  103.4 10.0 %collective-permute-done = bf16[2,1,256,512]{3,2,0,1:T(8,128)(2,1)S(1)} collective-permute-done((bf16[2,1,256,512]{3,2,0,1:T(8,128)(2,1)}, bf16[2,1,256,512]{3,2,0,1:T(8,128)(2,1)S(1)}, u32[]{:S(2)}, u32[]{:S(2)}) %collective-permute-start) | collective-permute-done | bytes 524320 | tf_op jit(solution)/shard_map/while/body/eval_jaxpr/ppermute | solution.py:10
  113.4 2.6 fusion.127
  116.0 1.9 collective-permute-start
  117.9 10.0 %collective-permute-done = bf16[2,1,256,512]{3,2,0,1:T(8,128)(2,1)S(1)} collective-permute-done((bf16[2,1,256,512]{3,2,0,1:T(8,128)(2,1)}, bf16[2,1,256,512]{3,2,0,1:T(8,128)(2,1)S(1)}, u32[]{:S(2)}, u32[]{:S(2)}) %collective-permute-start) | collective-permute-done | bytes 524320 | tf_op jit(solution)/shard_map/while/body/eval_jaxpr/ppermute | solution.py:10
  127.9 2.6 fusion.127
  130.5 1.9 collective-permute-start
  132.4 10.0 %collective-permute-done = bf16[2,1,256,512]{3,2,0,1:T(8,128)(2,1)S(1)} collective-permute-done((bf16[2,1,256,512]{3,2,0,1:T(8,128)(2,1)}, bf16[2,1,256,512]{3,2,0,1:T(8,128)(2,1)S(1)}, u32[]{:S(2)}, u32[]{:S(2)}) %collective-permute-start) | collective-permute-done | bytes 524320 | tf_op jit(solution)/shard_map/while/body/eval_jaxpr/ppermute | solution.py:10
  142.5 2.6 fusion.127
  145.0 1.9 collective-permute-start
  146.9 10.0 %collective-permute-done = bf16[2,1,256,512]{3,2,0,1:T(8,128)(2,1)S(1)} collective-permute-done((bf16[2,1,256,512]{3,2,0,1:T(8,128)(2,1)}, bf16[2,1,256,512]{3,2,0,1:T(8,128)(2,1)S(1)}, u32[]{:S(2)}, u32[]{:S(2)}) %collective-permute-start) | collective-permute-done | bytes 524320 | tf_op jit(solution)/shard_map/while/body/eval_jaxpr/ppermute | solution.py:10
  157.0 2.6 fusion.127
  159.5 1.9 collective-permute-start
  161.5 10.0 %collective-permute-done = bf16[2,1,256,512]{3,2,0,1:T(8,128)(2,1)S(1)} collective-permute-done((bf16[2,1,256,512]{3,2,0,1:T(8,128)(2,1)}, bf16[2,1,256,512]{3,2,0,1:T(8,128)(2,1)S(1)}, u32[]{:S(2)}, u32[]{:S(2)}) %collective-permute-start) | collective-permute-done | bytes 524320 | tf_op jit(solution)/shard_map/while/body/eval_jaxpr/ppermute | solution.py:10
  171.5 2.6 fusion.127
  174.0 1.9 collective-permute-start
  176.0 10.0 %collective-permute-done = bf16[2,1,256,512]{3,2,0,1:T(8,128)(2,1)S(1)} collective-permute-done((bf16[2,1,256,512]{3,2,0,1:T(8,128)(2,1)}, bf16[2,1,256,512]{3,2,0,1:T(8,128)(2,1)S(1)}, u32[]{:S(2)}, u32[]{:S(2)}) %collective-permute-start) | collective-permute-done | bytes 524320 | tf_op jit(solution)/shard_map/while/body/eval_jaxpr/ppermute | solution.py:10
  186.0 2.6 fusion.127
  188.6 1.9 collective-permute-start
  190.5 10.0 %collective-permute-done = bf16[2,1,256,512]{3,2,0,1:T(8,128)(2,1)S(1)} collective-permute-done((bf16[2,1,256,512]{3,2,0,1:T(8,128)(2,1)}, bf16[2,1,256,512]{3,2,0,1:T(8,128)(2,1)S(1)}, u32[]{:S(2)}, u32[]{:S(2)}) %collective-permute-start) | collective-permute-done | bytes 524320 | tf_op jit(solution)/shard_map/while/body/eval_jaxpr/ppermute | solution.py:10
  200.5 2.6 fusion.127
  203.1 1.9 collective-permute-start
  205.0 10.0 %collective-permute-done = bf16[2,1,256,512]{3,2,0,1:T(8,128)(2,1)S(1)} collective-permute-done((bf16[2,1,256,512]{3,2,0,1:T(8,128)(2,1)}, bf16[2,1,256,512]{3,2,0,1:T(8,128)(2,1)S(1)}, u32[]{:S(2)}, u32[]{:S(2)}) %collective-permute-start) | collective-permute-done | bytes 524320 | tf_op jit(solution)/shard_map/while/body/eval_jaxpr/ppermute | solution.py:10
  215.0 2.6 fusion.127
  217.6 1.9 collective-permute-start
  219.5 10.0 %collective-permute-done = bf16[2,1,256,512]{3,2,0,1:T(8,128)(2,1)S(1)} collective-permute-done((bf16[2,1,256,512]{3,2,0,1:T(8,128)(2,1)}, bf16[2,1,256,512]{3,2,0,1:T(8,128)(2,1)S(1)}, u32[]{:S(2)}, u32[]{:S(2)}) %collective-permute-start) | collective-permute-done | bytes 524320 | tf_op jit(solution)/shard_map/while/body/eval_jaxpr/ppermute | solution.py:10
  229.5 0.9 copy-done.4
  231.5 1.6 fusion.35
  233.2 1.5 maximum_bitcast_fusion.16
  236.7 0.9 copy.22
  237.6 7.0 %all-to-all-start.1 = ((bf16[1,2,2,128,256]{4,2,1,0,3:T(2,128)(2,1)}), bf16[1,2,2,128,256]{4,2,1,0,3:T(2,128)(2,1)S(1)}, u32[]{:S(2)}, u32[]{:S(2)}) async-start(bf16[1,2,2,128,256]{4,2,1,0,3:T(2,128)(2,1)} %copy.22), calls=%async_computation.1 | async-start | bytes 524288 | tf_op jit(solution)/shard_map/all_to_all | solution.py:112
  245.8 0.9 copy.19
  246.7 6.4 %all-to-all-done.1 = bf16[1,2,2,128,256]{4,2,1,0,3:T(2,128)(2,1)S(1)} async-done(((bf16[1,2,2,128,256]{4,2,1,0,3:T(2,128)(2,1)}), bf16[1,2,2,128,256]{4,2,1,0,3:T(2,128)(2,1)S(1)}, u32[]{:S(2)}, u32[]{:S(2)}) %all-to-all-start.1) | async-done | bytes 262176 | tf_op jit(solution)/shard_map/all_to_all | solution.py:112
  253.2 3.8 %all-to-all-start = ((bf16[1,2,2,128,256]{4,2,1,0,3:T(2,128)(2,1)}), bf16[1,2,2,128,256]{4,2,1,0,3:T(2,128)(2,1)S(1)}, u32[]{:S(2)}, u32[]{:S(2)}) async-start(bf16[1,2,2,128,256]{4,2,1,0,3:T(2,128)(2,1)} %copy.19), calls=%async_computation | async-start | bytes 524288 | tf_op jit(solution)/shard_map/all_to_all | solution.py:111
  257.0 8.4 %all-to-all-done = bf16[1,2,2,128,256]{4,2,1,0,3:T(2,128)(2,1)S(1)} async-done(((bf16[1,2,2,128,256]{4,2,1,0,3:T(2,128)(2,1)}), bf16[1,2,2,128,256]{4,2,1,0,3:T(2,128)(2,1)S(1)}, u32[]{:S(2)}, u32[]{:S(2)}) %all-to-all-start) | async-done | bytes 262176 | tf_op jit(solution)/shard_map/all_to_all | solution.py:111
  266.1 33.3 %while.25 = (s32[]{:T(128)}, bf16[16,2,2,8,256]{4,3,2,1,0:T(8,128)(2,1)S(1)}, bf16[16,2,2,8,256]{4,3,2,1,0:T(8,128)(2,1)S(1)}, s32[16]{0:T(128)S(1)}, bf16[48,2,...) while((s32[]{:T(128)}, ...), condition=%wide.region_5.6_spmd, body=%wide.region_2.5_spmd.sunk | while | flops 802822 | bytes 1654943 | solution.py:70
  299.3 11.9 %all_to_all.54 = bf16[16,2,2,8,256]{4,3,2,1,0:T(8,128)(2,1)S(1)} all-to-all(bf16[16,2,2,8,256]{4,3,2,1,0:T(8,128)(2,1)S(1)} %get-tuple-element.127), channel_id=1, replica_groups=mesh['energy'=16,'domain'=16] {'energy'}, dimensions={0} | all-to-all | bytes 524288 | tf_op jit(solution)/shard_map/all_to_all | solution.py:114
  (128 shorter events, 19.9 us)
Async XLA Ops:
  0.0 1.4 copy-start.2
  4.1 1.1 copy-start
  4.1 1.2 copy-start.1
  8.7 1.2 copy-start.3
  8.7 1.5 copy-start.5
  8.7 1.5 copy-start.6
  14.4 11.9 %collective-permute-start = (bf16[2,1,256,512]{3,2,0,1:T(8,128)(2,1)}, bf16[2,1,256,512]{3,2,0,1:T(8,128)(2,1)S(1)}, u32[]{:S(2)}, u32[]{:S(2)}) collective-permute-start(bf16[2,1,256,512]{3,2,0,1:T(8,128)(2,1)} %fusion.127), channel_id=1, source_target_pairs={{0,1},{1,2},{2,3},{3,4},{4,5},{5,6},{6,7},{7,8},{8,9},{9,10},{10,1... | collective-permute-start | bytes 1572872 | tf_op jit(solution)/shard_map/while/body/eval_jaxpr/ppermute | solution.py:10
  28.9 11.9 %collective-permute-start = (bf16[2,1,256,512]{3,2,0,1:T(8,128)(2,1)}, bf16[2,1,256,512]{3,2,0,1:T(8,128)(2,1)S(1)}, u32[]{:S(2)}, u32[]{:S(2)}) collective-permute-start(bf16[2,1,256,512]{3,2,0,1:T(8,128)(2,1)} %fusion.127), channel_id=1, source_target_pairs={{0,1},{1,2},{2,3},{3,4},{4,5},{5,6},{6,7},{7,8},{8,9},{9,10},{10,1... | collective-permute-start | bytes 1572872 | tf_op jit(solution)/shard_map/while/body/eval_jaxpr/ppermute | solution.py:10
  43.4 11.9 %collective-permute-start = (bf16[2,1,256,512]{3,2,0,1:T(8,128)(2,1)}, bf16[2,1,256,512]{3,2,0,1:T(8,128)(2,1)S(1)}, u32[]{:S(2)}, u32[]{:S(2)}) collective-permute-start(bf16[2,1,256,512]{3,2,0,1:T(8,128)(2,1)} %fusion.127), channel_id=1, source_target_pairs={{0,1},{1,2},{2,3},{3,4},{4,5},{5,6},{6,7},{7,8},{8,9},{9,10},{10,1... | collective-permute-start | bytes 1572872 | tf_op jit(solution)/shard_map/while/body/eval_jaxpr/ppermute | solution.py:10
  57.9 11.9 %collective-permute-start = (bf16[2,1,256,512]{3,2,0,1:T(8,128)(2,1)}, bf16[2,1,256,512]{3,2,0,1:T(8,128)(2,1)S(1)}, u32[]{:S(2)}, u32[]{:S(2)}) collective-permute-start(bf16[2,1,256,512]{3,2,0,1:T(8,128)(2,1)} %fusion.127), channel_id=1, source_target_pairs={{0,1},{1,2},{2,3},{3,4},{4,5},{5,6},{6,7},{7,8},{8,9},{9,10},{10,1... | collective-permute-start | bytes 1572872 | tf_op jit(solution)/shard_map/while/body/eval_jaxpr/ppermute | solution.py:10
  72.4 11.9 %collective-permute-start = (bf16[2,1,256,512]{3,2,0,1:T(8,128)(2,1)}, bf16[2,1,256,512]{3,2,0,1:T(8,128)(2,1)S(1)}, u32[]{:S(2)}, u32[]{:S(2)}) collective-permute-start(bf16[2,1,256,512]{3,2,0,1:T(8,128)(2,1)} %fusion.127), channel_id=1, source_target_pairs={{0,1},{1,2},{2,3},{3,4},{4,5},{5,6},{6,7},{7,8},{8,9},{9,10},{10,1... | collective-permute-start | bytes 1572872 | tf_op jit(solution)/shard_map/while/body/eval_jaxpr/ppermute | solution.py:10
  87.0 11.9 %collective-permute-start = (bf16[2,1,256,512]{3,2,0,1:T(8,128)(2,1)}, bf16[2,1,256,512]{3,2,0,1:T(8,128)(2,1)S(1)}, u32[]{:S(2)}, u32[]{:S(2)}) collective-permute-start(bf16[2,1,256,512]{3,2,0,1:T(8,128)(2,1)} %fusion.127), channel_id=1, source_target_pairs={{0,1},{1,2},{2,3},{3,4},{4,5},{5,6},{6,7},{7,8},{8,9},{9,10},{10,1... | collective-permute-start | bytes 1572872 | tf_op jit(solution)/shard_map/while/body/eval_jaxpr/ppermute | solution.py:10
  101.5 11.9 %collective-permute-start = (bf16[2,1,256,512]{3,2,0,1:T(8,128)(2,1)}, bf16[2,1,256,512]{3,2,0,1:T(8,128)(2,1)S(1)}, u32[]{:S(2)}, u32[]{:S(2)}) collective-permute-start(bf16[2,1,256,512]{3,2,0,1:T(8,128)(2,1)} %fusion.127), channel_id=1, source_target_pairs={{0,1},{1,2},{2,3},{3,4},{4,5},{5,6},{6,7},{7,8},{8,9},{9,10},{10,1... | collective-permute-start | bytes 1572872 | tf_op jit(solution)/shard_map/while/body/eval_jaxpr/ppermute | solution.py:10
  116.0 11.9 %collective-permute-start = (bf16[2,1,256,512]{3,2,0,1:T(8,128)(2,1)}, bf16[2,1,256,512]{3,2,0,1:T(8,128)(2,1)S(1)}, u32[]{:S(2)}, u32[]{:S(2)}) collective-permute-start(bf16[2,1,256,512]{3,2,0,1:T(8,128)(2,1)} %fusion.127), channel_id=1, source_target_pairs={{0,1},{1,2},{2,3},{3,4},{4,5},{5,6},{6,7},{7,8},{8,9},{9,10},{10,1... | collective-permute-start | bytes 1572872 | tf_op jit(solution)/shard_map/while/body/eval_jaxpr/ppermute | solution.py:10
  130.5 11.9 %collective-permute-start = (bf16[2,1,256,512]{3,2,0,1:T(8,128)(2,1)}, bf16[2,1,256,512]{3,2,0,1:T(8,128)(2,1)S(1)}, u32[]{:S(2)}, u32[]{:S(2)}) collective-permute-start(bf16[2,1,256,512]{3,2,0,1:T(8,128)(2,1)} %fusion.127), channel_id=1, source_target_pairs={{0,1},{1,2},{2,3},{3,4},{4,5},{5,6},{6,7},{7,8},{8,9},{9,10},{10,1... | collective-permute-start | bytes 1572872 | tf_op jit(solution)/shard_map/while/body/eval_jaxpr/ppermute | solution.py:10
  145.0 11.9 %collective-permute-start = (bf16[2,1,256,512]{3,2,0,1:T(8,128)(2,1)}, bf16[2,1,256,512]{3,2,0,1:T(8,128)(2,1)S(1)}, u32[]{:S(2)}, u32[]{:S(2)}) collective-permute-start(bf16[2,1,256,512]{3,2,0,1:T(8,128)(2,1)} %fusion.127), channel_id=1, source_target_pairs={{0,1},{1,2},{2,3},{3,4},{4,5},{5,6},{6,7},{7,8},{8,9},{9,10},{10,1... | collective-permute-start | bytes 1572872 | tf_op jit(solution)/shard_map/while/body/eval_jaxpr/ppermute | solution.py:10
  159.5 11.9 %collective-permute-start = (bf16[2,1,256,512]{3,2,0,1:T(8,128)(2,1)}, bf16[2,1,256,512]{3,2,0,1:T(8,128)(2,1)S(1)}, u32[]{:S(2)}, u32[]{:S(2)}) collective-permute-start(bf16[2,1,256,512]{3,2,0,1:T(8,128)(2,1)} %fusion.127), channel_id=1, source_target_pairs={{0,1},{1,2},{2,3},{3,4},{4,5},{5,6},{6,7},{7,8},{8,9},{9,10},{10,1... | collective-permute-start | bytes 1572872 | tf_op jit(solution)/shard_map/while/body/eval_jaxpr/ppermute | solution.py:10
  174.0 11.9 %collective-permute-start = (bf16[2,1,256,512]{3,2,0,1:T(8,128)(2,1)}, bf16[2,1,256,512]{3,2,0,1:T(8,128)(2,1)S(1)}, u32[]{:S(2)}, u32[]{:S(2)}) collective-permute-start(bf16[2,1,256,512]{3,2,0,1:T(8,128)(2,1)} %fusion.127), channel_id=1, source_target_pairs={{0,1},{1,2},{2,3},{3,4},{4,5},{5,6},{6,7},{7,8},{8,9},{9,10},{10,1... | collective-permute-start | bytes 1572872 | tf_op jit(solution)/shard_map/while/body/eval_jaxpr/ppermute | solution.py:10
  188.6 11.9 %collective-permute-start = (bf16[2,1,256,512]{3,2,0,1:T(8,128)(2,1)}, bf16[2,1,256,512]{3,2,0,1:T(8,128)(2,1)S(1)}, u32[]{:S(2)}, u32[]{:S(2)}) collective-permute-start(bf16[2,1,256,512]{3,2,0,1:T(8,128)(2,1)} %fusion.127), channel_id=1, source_target_pairs={{0,1},{1,2},{2,3},{3,4},{4,5},{5,6},{6,7},{7,8},{8,9},{9,10},{10,1... | collective-permute-start | bytes 1572872 | tf_op jit(solution)/shard_map/while/body/eval_jaxpr/ppermute | solution.py:10
  203.1 11.9 %collective-permute-start = (bf16[2,1,256,512]{3,2,0,1:T(8,128)(2,1)}, bf16[2,1,256,512]{3,2,0,1:T(8,128)(2,1)S(1)}, u32[]{:S(2)}, u32[]{:S(2)}) collective-permute-start(bf16[2,1,256,512]{3,2,0,1:T(8,128)(2,1)} %fusion.127), channel_id=1, source_target_pairs={{0,1},{1,2},{2,3},{3,4},{4,5},{5,6},{6,7},{7,8},{8,9},{9,10},{10,1... | collective-permute-start | bytes 1572872 | tf_op jit(solution)/shard_map/while/body/eval_jaxpr/ppermute | solution.py:10
  217.6 11.9 %collective-permute-start = (bf16[2,1,256,512]{3,2,0,1:T(8,128)(2,1)}, bf16[2,1,256,512]{3,2,0,1:T(8,128)(2,1)S(1)}, u32[]{:S(2)}, u32[]{:S(2)}) collective-permute-start(bf16[2,1,256,512]{3,2,0,1:T(8,128)(2,1)} %fusion.127), channel_id=1, source_target_pairs={{0,1},{1,2},{2,3},{3,4},{4,5},{5,6},{6,7},{7,8},{8,9},{9,10},{10,1... | collective-permute-start | bytes 1572872 | tf_op jit(solution)/shard_map/while/body/eval_jaxpr/ppermute | solution.py:10
  229.5 1.0 copy-start.4
  229.5 1.0 copy-start.7
  229.5 1.0 copy-start.8
  235.5 0.7 copy-start.9
  237.6 15.6 %all-to-all-start.1 = ((bf16[1,2,2,128,256]{4,2,1,0,3:T(2,128)(2,1)}), bf16[1,2,2,128,256]{4,2,1,0,3:T(2,128)(2,1)S(1)}, u32[]{:S(2)}, u32[]{:S(2)}) async-start(bf16[1,2,2,128,256]{4,2,1,0,3:T(2,128)(2,1)} %copy.22), calls=%async_computation.1 | async-start | bytes 524288 | tf_op jit(solution)/shard_map/all_to_all | solution.py:112
  253.2 12.2 %all-to-all-start = ((bf16[1,2,2,128,256]{4,2,1,0,3:T(2,128)(2,1)}), bf16[1,2,2,128,256]{4,2,1,0,3:T(2,128)(2,1)S(1)}, u32[]{:S(2)}, u32[]{:S(2)}) async-start(bf16[1,2,2,128,256]{4,2,1,0,3:T(2,128)(2,1)} %copy.19), calls=%async_computation | async-start | bytes 524288 | tf_op jit(solution)/shard_map/all_to_all | solution.py:111
  265.4 0.7 copy-start.10
where the time goes:
time: 314 us; the launch traced here: 312 us
  waiting for transfers between devices  165 us (53%)
  matrix products  47.5 us (15%)
  starting transfers between devices  39.4 us (13%)
  loops' own time  21.6 us (7%)
  local copies, waits for them, and re-layouts  20 us (6%)
  blocking collectives  11.9 us (4%)
  other arithmetic  6.47 us (2%)
    ppermute x15, waiting for transfers between devices, passed_along(): return lax.ppermute(block, axis, route)  150 us
    dot_general x19, matrix products, product_adjoint(): jnp.matmul(factor, jnp.swapaxes(stacked(second), -1, -2), preferred_eleme...  45.7 us
    ppermute x15, starting transfers between devices, passed_along(): return lax.ppermute(block, axis, route)  28.6 us
    another operation x1, loops' own time, convolve(): return lax.map(one_output, offsets)  21.4 us
    all_to_all x1, blocking collectives, shards(): lax.all_to_all(result, 'energy', split_axis=0, concat_axis=3, tiled=True)  11.9 us
    dynamic_slice x16, local copies, waits for them, and re-layouts, convolve(): return lax.map(one_output, offsets)  9.38 us
    all_to_all x1, waiting for transfers between devices, shards(): lax.all_to_all(chosen_less, 'energy', split_axis=3, concat_axis=0, tiled=...  8.43 us
    all_to_all x1, starting transfers between devices, shards(): lax.all_to_all(chosen_great, 'energy', split_axis=3, concat_axis=0, tiled...  7.04 us
  transfers between devices with their start and end apart: 17, of which 17 were waited for; matrix products, arithmetic and copies ran while one was open for 1% of the time, Pallas kernels for 0%

commit v1 on v0

v1 whole, which is shorter than its diff:
```python
import jax
import jax.numpy as jnp
from jax import lax
from jax.experimental import pallas as pl
from jax.experimental.pallas import tpu as pltpu
from jax.sharding import PartitionSpec as P

MESH = pl.DeviceIdType.MESH
BF = jnp.bfloat16
F32 = jnp.float32


def stacked(x):
    n = x.shape[1] // 2
    re, im = x[:, :n], x[:, n:]
    return jnp.concatenate([x, jnp.concatenate([-im, re], axis=1)], axis=0)


def mul(a, x):
    return jnp.dot(a, stacked(x), preferred_element_type=F32)


def mul_adj(y, a):
    return lax.dot_general(y, stacked(a), (((1,), (1,)), ((), ())), preferred_element_type=F32)


def congruence(t, s):
    return mul_adj(mul(t, s).astype(BF), t)


def kernel(ret, cpl, sl, sg, tiles_hbm, offs, out,
           R, C, SG, PP, T, J, JX, Q, A1, A2, S1, S2, S3, TB, SB, AB, LF, GF, OB, tl,
           ld, sp, rp, sj, rj, sa, ra, ss, rs, st, rt, sx, rx, so, ro):
    e = lax.axis_index("energy")
    d = lax.axis_index("domain")
    c, q = lax.div(d, 2), lax.rem(d, 2)
    peer = 2 * c + 1 - q

    def remote(src, dst, send, recv, ee, dd):
        return pltpu.make_async_remote_copy(src_ref=src, dst_ref=dst, send_sem=send, recv_sem=recv,
                                            device_id=(ee, dd), device_id_type=MESH)

    def at_chip(k):
        return 2 * k + q

    bar = pltpu.get_barrier_semaphore()
    for k in range(1, 8):
        pl.semaphore_signal(bar, 1, device_id=(e, at_chip(lax.rem(c + k, 8))), device_id_type=MESH)
    pl.semaphore_signal(bar, 1, device_id=(e, peer), device_id_type=MESH)
    for k in range(1, 16):
        for z in range(2):
            pl.semaphore_signal(bar, 1, device_id=(lax.rem(e + k, 16), 2 * c + z), device_id_type=MESH)

    loads = []
    for b in range(2):
        for n, (src, dst) in enumerate(((ret.at[0, b], R.at[b]), (cpl.at[b], C.at[b]),
                                        (sl.at[0, b], SG.at[0, b]), (sg.at[0, b], SG.at[1, b]))):
            cp = pltpu.make_async_copy(src, dst, ld.at[4 * b + n])
            cp.start()
            loads.append(cp)
    own_tiles = pltpu.make_async_copy(tiles_hbm, tl.at[q], ld.at[8])
    own_tiles.start()

    for b in range(2):
        loads[4 * b].wait()
        loads[4 * b + 1].wait()
        PP[2 * q + b] = mul(R[b], C[b]).astype(BF)
    pl.semaphore_wait(bar, 7 + 1 + 30)
    p_copy = remote(PP.at[pl.ds(2 * q, 2)], PP.at[pl.ds(2 * q, 2)], sp, rp, e, peer)
    p_copy.start()
    own_tiles.wait()
    t_copy = remote(tl.at[q], tl.at[q], st.at[1], rt.at[1], e, peer)
    t_copy.start()

    for b in range(2):
        loads[4 * b + 2].wait()
        loads[4 * b + 3].wait()
        JX[b] = mul_adj(mul(R[b], SG[1 - q, b]).astype(BF), R[b]).astype(BF)
    j_copy = remote(JX, J.at[pl.ds(2 * q, 2)], sj, rj, e, peer)
    j_copy.start()
    for b in range(2):
        J[2 * q + b] = mul_adj(mul(R[b], SG[q, b]).astype(BF), R[b]).astype(BF)

    p_copy.wait_recv()
    T[0] = PP[0]
    for i in range(1, 4):
        T[i] = mul(PP[i], T[i - 1]).astype(BF)
    half = pl.ds(pl.multiple_of(128 * q, 128), 128)
    a1 = remote(T.at[3, half], A1.at[half], sa.at[0], ra.at[0], e, at_chip(lax.rem(c + 1, 8)))
    a1f = remote(A1.at[half], A1.at[half], sa.at[1], ra.at[1], e, peer)
    a1_sender = (lax.rem(c, 2) == 0) & (c > 0)
    a1_taker = (lax.rem(c, 2) == 1) & (c > 1)

    @pl.when(a1_sender)
    def _():
        a1.start()

    j_copy.wait_recv()
    Q[0] = J[0]
    for i in range(1, 4):
        Q[i] = (congruence(PP[i], Q[i - 1]) + J[i].astype(F32)).astype(BF)

    even = lax.rem(c, 2) == 0
    s1 = remote(Q.at[3], S1, ss.at[0], rs.at[0], e, at_chip(lax.rem(c + 1, 8)))

    @pl.when(even)
    def _():
        s1.start()

    def update(i, slot, s_ref):
        Q[i] = (Q[i].astype(F32) + congruence(T[4 * slot + i], s_ref[...])).astype(BF)

    a2a = remote(T.at[7, half], A2.at[half], sa.at[2], ra.at[2], e, at_chip(lax.rem(c + 2, 8)))
    a2b = remote(T.at[7, half], A2.at[half], sa.at[3], ra.at[2], e, at_chip(lax.rem(c + 1, 8)))
    a2f = remote(A2.at[half], A2.at[half], sa.at[4], ra.at[3], e, peer)

    @pl.when(a1_taker)
    def _():
        a1.wait_recv()
        a1f.start()
        a1f.wait_recv()
        a_in = stacked(A1[...])
        for i in (3, 0, 1, 2):
            T[4 + i] = jnp.dot(T[i], a_in, preferred_element_type=F32).astype(BF)
            if i == 3:
                @pl.when(c == 5)
                def _():
                    a2a.start()
                    a2b.start()

    s2a = remote(Q.at[3], S2, ss.at[1], rs.at[1], e, at_chip(lax.rem(c + 2, 8)))
    s2b = remote(Q.at[3], S2, ss.at[2], rs.at[1], e, at_chip(lax.rem(c + 1, 8)))
    s2_sender = (c == 1) | (c == 5)

    @pl.when(jnp.logical_not(even))
    def _():
        s1.wait_recv()
        update(3, 0, S1)

        @pl.when(s2_sender)
        def _():
            s2a.start()
            s2b.start()

        for i in range(3):
            update(i, 0, S1)

    slot2 = lax.rem(c, 2)

    @pl.when(c >= 6)
    def _():
        a2a.wait_recv()
        a2f.start()
        a2f.wait_recv()
        a_in = stacked(A2[...])
        for i in range(4):
            T[8 + i] = jnp.dot(T[4 * slot2 + i], a_in, preferred_element_type=F32).astype(BF)

    @pl.when(even)
    def _():
        s1.wait_send()

    s3a = remote(Q.at[3], S3, ss.at[3], rs.at[2], e, at_chip(lax.rem(c + 2, 8)))
    s3b = remote(Q.at[3], S3, ss.at[4], rs.at[2], e, at_chip(lax.rem(c + 4, 8)))
    s3c = remote(S3, S3, ss.at[3], rs.at[2], e, at_chip(lax.rem(c + 1, 8)))
    s3d = remote(S3, S3, ss.at[4], rs.at[2], e, at_chip(lax.rem(c + 7, 8)))

    @pl.when(lax.rem(lax.div(c, 2), 2) == 1)
    def _():
        s2a.wait_recv()
        update(3, slot2, S2)

        @pl.when(c == 3)
        def _():
            s3a.start()
            s3b.start()

        for i in range(3):
            update(i, slot2, S2)

    @pl.when(s2_sender)
    def _():
        s2a.wait_send()
        s2b.wait_send()

    slot3 = jnp.where(c >= 6, 2, slot2)

    @pl.when(c >= 4)
    def _():
        s3a.wait_recv()

        @pl.when(c == 5)
        def _():
            s3c.start()
            s3d.start()

        for i in range(4):
            update(i, slot3, S3)

    t_copy.wait_recv()
    for i in range(4):
        for t in range(4):
            row, col = 128 * (t // 2), 128 * (t % 2)
            TB[4 * i + t, :, 0:128] = Q[i, row:row + 128, col:col + 128]
            TB[4 * i + t, :, 128:256] = Q[i, row:row + 128, col + 256:col + 384]
    for i in range(4):
        for j in range(2):
            tile = TB[4 * i + tl[i // 2, i % 2, j]]
            for r in range(4):
                SB[8 * i + 4 * j + r] = tile[32 * r:32 * r + 32]

    mine = pltpu.make_async_copy(SB.at[2 * e + q], AB.at[q, e], rx)
    mine.start()
    remote(SB.at[2 * e + 1 - q], AB.at[q, e], sx, rx, e, peer).start()
    for k in range(1, 16):
        o = lax.rem(e + k, 16)
        for z in range(2):
            remote(SB.at[2 * o + z], AB.at[q, e], sx, rx, o, 2 * c + z).start()
    GF[0:8] = jnp.zeros((8, 32, 256), F32)
    GF[24:32] = jnp.zeros((8, 32, 256), F32)
    pltpu.make_async_copy(AB, AB, rx).wait()
    pltpu.make_async_copy(SB.at[pl.ds(0, 31)], SB.at[pl.ds(0, 31)], sx).wait()

    for k in range(16):
        GF[8 + k] = AB[1, k].astype(F32)
    for rr in range(4):
        rows = pl.ds(8 * rr, 8)
        lr, li = [], []
        for k in range(16):
            v = AB[0, k, pl.ds(8 * rr, 8), :].astype(F32)
            lr.append(v[:, :128])
            li.append(v[:, 128:])
        for k in range(16):
            LF[k, rows, :] = jnp.concatenate([lr[k], li[k]], axis=1)

    def one(m, carry):
        base = 8 - offs[m]
        for rr in range(4):
            rows = pl.ds(8 * rr, 8)
            acc_r = jnp.zeros((8, 128), F32)
            acc_i = jnp.zeros((8, 128), F32)
            for k in range(16):
                lr = LF[k, rows, 0:128]
                li = LF[k, rows, 128:256]
                gr = GF[base + k, rows, 0:128]
                gi = GF[base + k, rows, 128:256]
                acc_r = acc_r + (lr * gr - li * gi)
                acc_i = acc_i + (lr * gi + li * gr)
            OB[m, rows, 0:128] = (acc_r * (1.0 / 16)).astype(BF)
            OB[m, rows, 128:256] = (acc_i * (1.0 / 16)).astype(BF)
        return carry

    lax.fori_loop(0, 16, one, 0)

    u, h = lax.div(e, 2), lax.rem(e, 2)
    blk, j = lax.div(u, 2), lax.rem(u, 2)
    home = lax.div(blk, 2)
    dst = out.at[0, lax.rem(blk, 2), j, pl.ds(pl.multiple_of(h * 64 + q * 32, 32), 32), :]
    is_home = home == q

    @pl.when(is_home)
    def _():
        pltpu.make_async_copy(OB.at[e], dst, ro).start()

    @pl.when(jnp.logical_not(is_home))
    def _():
        remote(OB.at[e], dst, so, ro, e, peer).start()

    for k in range(1, 16):
        m = lax.rem(e + k, 16)
        remote(OB.at[m], dst, so, ro, m, 2 * c + home).start()
    pltpu.make_async_copy(out, out, ro).wait()

    @pl.when(is_home)
    def _():
        pltpu.make_async_copy(OB.at[pl.ds(0, 15)], OB.at[pl.ds(0, 15)], so).wait()

    @pl.when(jnp.logical_not(is_home))
    def _():
        pltpu.make_async_copy(OB, OB, so).wait()

    p_copy.wait_send()
    t_copy.wait_send()
    j_copy.wait_send()

    @pl.when(a1_sender)
    def _():
        a1.wait_send()

    @pl.when(a1_taker)
    def _():
        a1f.wait_send()

    @pl.when(c == 5)
    def _():
        a2a.wait_send()
        a2b.wait_send()
        s3c.wait_send()
        s3d.wait_send()

    @pl.when(c >= 6)
    def _():
        a2f.wait_send()

    @pl.when(c == 3)
    def _():
        s3a.wait_send()
        s3b.wait_send()


def shards(retarded, coupling, sigma_lesser, sigma_greater, tiles, offsets):
    mat = (256, 512)
    dma = pltpu.SemaphoreType.DMA
    anyspace = pl.BlockSpec(memory_space=pltpu.HBM)
    return pl.pallas_call(
        kernel,
        out_shape=jax.ShapeDtypeStruct((1, 2, 2, 128, 256), BF),
        in_specs=[anyspace] * 5 + [pl.BlockSpec(memory_space=pltpu.SMEM)],
        out_specs=pl.BlockSpec(memory_space=pltpu.VMEM),
        scratch_shapes=[
            pltpu.VMEM((2,) + mat, BF), pltpu.VMEM((2,) + mat, BF), pltpu.VMEM((2, 2) + mat, BF),
            pltpu.VMEM((4,) + mat, BF), pltpu.VMEM((12,) + mat, BF), pltpu.VMEM((4,) + mat, BF),
            pltpu.VMEM((2,) + mat, BF), pltpu.VMEM((4,) + mat, BF),
            pltpu.VMEM(mat, BF), pltpu.VMEM(mat, BF),
            pltpu.VMEM(mat, BF), pltpu.VMEM(mat, BF), pltpu.VMEM(mat, BF),
            pltpu.VMEM((16, 128, 256), BF), pltpu.VMEM((32, 32, 256), BF), pltpu.VMEM((2, 16, 32, 256), BF),
            pltpu.VMEM((16, 32, 256), F32), pltpu.VMEM((32, 32, 256), F32), pltpu.VMEM((16, 32, 256), BF),
            pltpu.SMEM((2, 2, 2), jnp.int32),
            dma((9,)), dma, dma, dma, dma, dma((5,)), dma((4,)), dma((5,)), dma((3,)), dma((2,)), dma((2,)),
            dma, dma, dma, dma,
        ],
        compiler_params=pltpu.CompilerParams(
            collective_id=0, has_side_effects=True, vmem_limit_bytes=48 << 20),
        name="recursion",
    )(retarded, coupling, sigma_lesser, sigma_greater, tiles, offsets)


def solution(mesh):
    placed = (
        P("energy", "domain", None, None),
        P("domain", None, None),
        P("energy", "domain", None, None),
        P("energy", "domain", None, None),
        P("domain", None),
        P(),
    )
    return jax.shard_map(
        shards,
        mesh=mesh,
        in_specs=placed,
        out_specs=P("energy", "domain", None, None, None),
        check_vma=False,
    )
```

time: 314 us -> 65.5 us (0.21)
  the two profiles are of different devices: /device:TPU:128 before, /device:TPU:129 now
where the time goes in v1:
time: 65.5 us; the launch traced here: 65.2 us
  Pallas kernels  59 us (90%)
  local copies, waits for them, and re-layouts  6.2 us (9%)
    pallas_call x1, Pallas kernels, shards(): pl.pallas_call(kernel, out_shape=jax.ShapeDtypeStruct((1, 2, 2, 128, 256)...  59 us
    unnamed x13, local copies, waits for them, and re-layouts  6.2 us

profile of v1, /device:TPU:129, one launch (start us, length us, event | category | flops | bytes accessed | tf_op | source)
XLA Modules:
  0.0 65.2 jit_solution(4317948490616614030)
XLA Ops:
  0.0 0.0 copy-start
  0.0 1.0 %copy-done = bf16[1,2,256,512]{3,2,1,0:T(8,128)(2,1)S(1)} copy-done((bf16[1,2,256,512]{3,2,1,0:T(8,128)(2,1)S(1)}, bf16[1,2,256,512]{3,2,1,0:T(8,128)(2,1)}, u32[]{:S(2)}) %copy-start) | copy-done | bytes 524312
  1.0 0.0 copy-start.1
  1.0 1.0 %copy-done.1 = bf16[2,256,512]{2,1,0:T(8,128)(2,1)S(1)} copy-done((bf16[2,256,512]{2,1,0:T(8,128)(2,1)S(1)}, bf16[2,256,512]{2,1,0:T(8,128)(2,1)}, u32[]{:S(2)}) %copy-start.1) | copy-done | bytes 524312
  2.1 0.0 copy-start.2
  2.1 1.0 %copy-done.2 = bf16[1,2,256,512]{3,2,1,0:T(8,128)(2,1)S(1)} copy-done((bf16[1,2,256,512]{3,2,1,0:T(8,128)(2,1)S(1)}, bf16[1,2,256,512]{3,2,1,0:T(8,128)(2,1)}, u32[]{:S(2)}) %copy-start.2) | copy-done | bytes 524312
  3.1 0.0 copy-start.3
  3.1 1.0 %copy-done.3 = bf16[1,2,256,512]{3,2,1,0:T(8,128)(2,1)S(1)} copy-done((bf16[1,2,256,512]{3,2,1,0:T(8,128)(2,1)S(1)}, bf16[1,2,256,512]{3,2,1,0:T(8,128)(2,1)}, u32[]{:S(2)}) %copy-start.3) | copy-done | bytes 524312
  4.2 0.0 copy-start.4
  4.2 0.7 %copy-done.4 = s32[2,2]{1,0:T(2,128)S(1)} copy-done((s32[2,2]{1,0:T(2,128)S(1)}, s32[2,2]{1,0:T(2,128)}, u32[]{:S(2)}) %copy-start.4) | copy-done | bytes 40
  4.8 0.0 copy-start.5
  4.9 0.7 %copy-done.5 = s32[16]{0:T(128)S(1)} copy-done((s32[16]{0:T(128)S(1)}, s32[16]{0:T(128)}, u32[]{:S(2)}) %copy-start.5) | copy-done | bytes 88
  5.5 59.0 %recursion.1 = bf16[1,2,2,128,256]{4,3,2,1,0:T(8,128)(2,1)S(1)} custom-call(bf16[1,2,256,512]{3,2,1,0:T(8,128)(2,1)S(1)} %copy-done, bf16[2,256,512]{2,1,0:T(8,128)(2,1)S(1)} %copy-done.1, bf16[1,2,256,512]{3,2,1,0:T(8,128)(2,1)S(1)} %copy-done.2, bf16[1,2,256,512]{3,2,1,0:T(8,128)(2,1)S(1)} %copy-done.3, s32[2,2]{1,0:T(2,128)S(1)} %copy-done.4, s32[16]{0:T(128)S(1)} %copy-done.5), custom_call_target="tpu_custom_call" | custom-call | tf_op jit(solution)/shard_map/recursion/pallas_call | solution.py:315
  64.5 0.7 %copy.8 = bf16[1,2,2,128,256]{4,3,2,1,0:T(8,128)(2,1)} copy(bf16[1,2,2,128,256]{4,3,2,1,0:T(8,128)(2,1)S(1)} %recursion.1) | data formatting | bytes 524288
Async XLA Ops:
  0.0 1.0 %copy-start = (bf16[1,2,256,512]{3,2,1,0:T(8,128)(2,1)S(1)}, bf16[1,2,256,512]{3,2,1,0:T(8,128)(2,1)}, u32[]{:S(2)}) copy-start(bf16[1,2,256,512]{3,2,1,0:T(8,128)(2,1)} %ret.1) | copy-start | bytes 1572868
  1.0 1.0 %copy-start.1 = (bf16[2,256,512]{2,1,0:T(8,128)(2,1)S(1)}, bf16[2,256,512]{2,1,0:T(8,128)(2,1)}, u32[]{:S(2)}) copy-start(bf16[2,256,512]{2,1,0:T(8,128)(2,1)} %cpl.1) | copy-start | bytes 1572868
  2.1 1.0 %copy-start.2 = (bf16[1,2,256,512]{3,2,1,0:T(8,128)(2,1)S(1)}, bf16[1,2,256,512]{3,2,1,0:T(8,128)(2,1)}, u32[]{:S(2)}) copy-start(bf16[1,2,256,512]{3,2,1,0:T(8,128)(2,1)} %sl.1) | copy-start | bytes 1572868
  3.1 1.0 %copy-start.3 = (bf16[1,2,256,512]{3,2,1,0:T(8,128)(2,1)S(1)}, bf16[1,2,256,512]{3,2,1,0:T(8,128)(2,1)}, u32[]{:S(2)}) copy-start(bf16[1,2,256,512]{3,2,1,0:T(8,128)(2,1)} %sg.1) | copy-start | bytes 1572868
  4.2 0.7 %copy-start.4 = (s32[2,2]{1,0:T(2,128)S(1)}, s32[2,2]{1,0:T(2,128)}, u32[]{:S(2)}) copy-start(s32[2,2]{1,0:T(2,128)} %tiles_hbm.1) | copy-start | bytes 52
  4.8 0.7 %copy-start.5 = (s32[16]{0:T(128)S(1)}, s32[16]{0:T(128)}, u32[]{:S(2)}) copy-start(s32[16]{0:T(128)} %offs.1) | copy-start | bytes 196

commit v2 on v1

--- a/solution.py
+++ b/solution.py
@@ -29,8 +29,8 @@
 
 
 def kernel(ret, cpl, sl, sg, tiles_hbm, offs, out,
-           R, C, SG, PP, T, J, JX, Q, A1, A2, S1, S2, S3, TB, SB, AB, LF, GF, OB, tl,
-           ld, sp, rp, sj, rj, sa, ra, ss, rs, st, rt, sx, rx, so, ro):
+           R, C, SG, PP, T, J, JX, Q, A1, A2, S1, S2, S3, AD, SD, SE, ZB, X3, TB, SB, AB, LF, GF, OB, tl,
+           ld, sp, rp, sj, rj, sa, ra, ss, rs, sd, rd, st, rt, sx3, rx3, sx, rx, so, ro):
     e = lax.axis_index("energy")
     d = lax.axis_index("domain")
     c, q = lax.div(d, 2), lax.rem(d, 2)
@@ -42,14 +42,6 @@
 
     def at_chip(k):
         return 2 * k + q
-
-    bar = pltpu.get_barrier_semaphore()
-    for k in range(1, 8):
-        pl.semaphore_signal(bar, 1, device_id=(e, at_chip(lax.rem(c + k, 8))), device_id_type=MESH)
-    pl.semaphore_signal(bar, 1, device_id=(e, peer), device_id_type=MESH)
-    for k in range(1, 16):
-        for z in range(2):
-            pl.semaphore_signal(bar, 1, device_id=(lax.rem(e + k, 16), 2 * c + z), device_id_type=MESH)
 
     loads = []
     for b in range(2):
@@ -60,6 +52,14 @@
             loads.append(cp)
     own_tiles = pltpu.make_async_copy(tiles_hbm, tl.at[q], ld.at[8])
     own_tiles.start()
+
+    bar = pltpu.get_barrier_semaphore()
+    for k in range(1, 8):
+        pl.semaphore_signal(bar, 1, device_id=(e, at_chip(lax.rem(c + k, 8))), device_id_type=MESH)
+    pl.semaphore_signal(bar, 1, device_id=(e, peer), device_id_type=MESH)
+    for k in range(1, 16):
+        for z in range(2):
+            pl.semaphore_signal(bar, 1, device_id=(lax.rem(e + k, 16), 2 * c + z), device_id_type=MESH)
 
     for b in range(2):
         loads[4 * b].wait()
@@ -81,6 +81,14 @@
     for b in range(2):
         J[2 * q + b] = mul_adj(mul(R[b], SG[q, b]).astype(BF), R[b]).astype(BF)
 
+    even = lax.rem(c, 2) == 0
+    rows2 = (pl.ds(0, 128), pl.ds(128, 128))
+    low_greater = (c < 4) & (q == 1)
+    below = at_chip(lax.rem(c + 7, 8))
+    down_sender = low_greater & jnp.logical_not(even)
+    down_taker = low_greater & even
+    ad = remote(T.at[3], AD, sd.at[0], rd.at[0], e, below)
+
     p_copy.wait_recv()
     T[0] = PP[0]
     for i in range(1, 4):
@@ -95,23 +103,74 @@
     def _():
         a1.start()
 
+    @pl.when(down_sender)
+    def _():
+        ad.start()
+
     j_copy.wait_recv()
     Q[0] = J[0]
     for i in range(1, 4):
         Q[i] = (congruence(PP[i], Q[i - 1]) + J[i].astype(F32)).astype(BF)
 
-    even = lax.rem(c, 2) == 0
     s1 = remote(Q.at[3], S1, ss.at[0], rs.at[0], e, at_chip(lax.rem(c + 1, 8)))
 
-    @pl.when(even)
+    dn = remote(Q.at[3], SD, sd.at[1], rd.at[1], e, below)
+    ae = remote(A2, A2, sd.at[2], rd.at[2], e, at_chip(lax.rem(c + 6, 8)))
+    ze = remote(ZB, SE, sd.at[3], rd.at[3], e, at_chip(lax.rem(c + 6, 8)))
+    z2 = [remote(ZB.at[r], S2.at[r], ss.at[2 * n + 1 + p], rs.at[1 + p], e, at_chip(lax.rem(c + dist, 8)))
+          for n, dist in enumerate((3, 2)) for p, r in enumerate(rows2)]
+
+    def chip_at(distance):
+        return at_chip(lax.rem(c + distance * (1 - 2 * q) + 16, 8))
+
+    x3 = [[remote(X3.at[r], S3.at[r], sx3.at[2 * n + p], rx3.at[p], e, chip_at(dist)) for p, r in enumerate(rows2)]
+          for n, dist in enumerate((3, 2, 1))]
+    hop = [remote(S3.at[r], S3.at[r], sx3.at[p], rx3.at[p], e, chip_at(1)) for p, r in enumerate(rows2)]
+    relay = c == jnp.where(q == 0, 6, 5)
+
+    @pl.when(even & jnp.logical_not(low_greater))
     def _():
         s1.start()
+
+    @pl.when(down_sender)
+    def _():
+        dn.start()
+
+    @pl.when(down_taker)
+    def _():
+        ad.wait_recv()
+
+        @pl.when(c == 2)
+        def _():
+            A2[...] = mul(AD[...], T[3]).astype(BF)
+            ae.start()
+
+        dn.wait_recv()
+        ZB[...] = (congruence(AD[...], Q[3]) + SD[...].astype(F32)).astype(BF)
+
+        @pl.when(c == 2)
+        def _():
+            ze.start()
+            ze.wait_send()
+
+        s1.start()
+
+        @pl.when(c == 0)
+        def _():
+            ae.wait_recv()
+            for cp in z2:
+                cp.start()
+            ze.wait_recv()
+            X3[...] = (congruence(A2[...], ZB[...]) + SE[...].astype(F32)).astype(BF)
+            for to in x3:
+                for cp in to:
+                    cp.start()
 
     def update(i, slot, s_ref):
         Q[i] = (Q[i].astype(F32) + congruence(T[4 * slot + i], s_ref[...])).astype(BF)
 
-    a2a = remote(T.at[7, half], A2.at[half], sa.at[2], ra.at[2], e, at_chip(lax.rem(c + 2, 8)))
-    a2b = remote(T.at[7, half], A2.at[half], sa.at[3], ra.at[2], e, at_chip(lax.rem(c + 1, 8)))
+    a2b = remote(T.at[7, half], A2.at[half], sa.at[2], ra.at[2], e, at_chip(lax.rem(c + 1, 8)))
+    a2r = remote(A2.at[half], A2.at[half], sa.at[3], ra.at[2], e, at_chip(lax.rem(c + 1, 8)))
     a2f = remote(A2.at[half], A2.at[half], sa.at[4], ra.at[3], e, peer)
 
     @pl.when(a1_taker)
@@ -125,32 +184,56 @@
             if i == 3:
                 @pl.when(c == 5)
                 def _():
-                    a2a.start()
                     a2b.start()
 
-    s2a = remote(Q.at[3], S2, ss.at[1], rs.at[1], e, at_chip(lax.rem(c + 2, 8)))
-    s2b = remote(Q.at[3], S2, ss.at[2], rs.at[1], e, at_chip(lax.rem(c + 1, 8)))
-    s2_sender = (c == 1) | (c == 5)
+    s2_low = (c == 1) & (q == 0)
+    far = at_chip(lax.rem(c + jnp.where(c == 1, 2, 1), 8))
+    s2a = [remote(Q.at[3, r], S2.at[r], ss.at[1 + p], rs.at[1 + p], e, far) for p, r in enumerate(rows2)]
+    s2b = [remote(Q.at[3, r], S2.at[r], ss.at[3 + p], rs.at[1 + p], e, at_chip(lax.rem(c + 1, 8)))
+           for p, r in enumerate(rows2)]
+    s2r = [remote(S2.at[r], S2.at[r], ss.at[1 + p], rs.at[1 + p], e, at_chip(lax.rem(c + 1, 8)))
+           for p, r in enumerate(rows2)]
+    s2_sender = s2_low | (c == 5)
 
     @pl.when(jnp.logical_not(even))
     def _():
         s1.wait_recv()
+
+        @pl.when(down_sender)
+        def _():
+            dn.wait_send()
+
         update(3, 0, S1)
 
         @pl.when(s2_sender)
         def _():
-            s2a.start()
-            s2b.start()
+            for cp in s2a:
+                cp.start()
 
         for i in range(3):
             update(i, 0, S1)
 
+        @pl.when(s2_sender)
+        def _():
+            for cp in s2a:
+                cp.wait_send()
+
+        @pl.when(s2_low)
+        def _():
+            for cp in s2b:
+                cp.start()
+
     slot2 = lax.rem(c, 2)
 
     @pl.when(c >= 6)
     def _():
-        a2a.wait_recv()
+        a2b.wait_recv()
         a2f.start()
+
+        @pl.when(c == 6)
+        def _():
+            a2r.start()
+
         a2f.wait_recv()
         a_in = stacked(A2[...])
         for i in range(4):
@@ -160,62 +243,73 @@
     def _():
         s1.wait_send()
 
-    s3a = remote(Q.at[3], S3, ss.at[3], rs.at[2], e, at_chip(lax.rem(c + 2, 8)))
-    s3b = remote(Q.at[3], S3, ss.at[4], rs.at[2], e, at_chip(lax.rem(c + 4, 8)))
-    s3c = remote(S3, S3, ss.at[3], rs.at[2], e, at_chip(lax.rem(c + 1, 8)))
-    s3d = remote(S3, S3, ss.at[4], rs.at[2], e, at_chip(lax.rem(c + 7, 8)))
-
     @pl.when(lax.rem(lax.div(c, 2), 2) == 1)
     def _():
-        s2a.wait_recv()
+        for cp, on in zip(s2a, s2r):
+            cp.wait_recv()
+
+            @pl.when(c == 6)
+            def _(on=on):
+                on.start()
+
         update(3, slot2, S2)
 
-        @pl.when(c == 3)
-        def _():
-            s3a.start()
-            s3b.start()
+        @pl.when((c == 3) & (q == 0))
+        def _():
+            X3[...] = Q[3]
+            for to in x3:
+                for cp in to:
+                    cp.start()
 
         for i in range(3):
             update(i, slot2, S2)
 
-    @pl.when(s2_sender)
-    def _():
-        s2a.wait_send()
-        s2b.wait_send()
+    @pl.when(s2_low)
+    def _():
+        for cp in s2b:
+            cp.wait_send()
 
     slot3 = jnp.where(c >= 6, 2, slot2)
 
     @pl.when(c >= 4)
     def _():
-        s3a.wait_recv()
-
-        @pl.when(c == 5)
-        def _():
-            s3c.start()
-            s3d.start()
-
-        for i in range(4):
+        for cp in hop:
+            cp.wait_recv()
+
+            @pl.when(relay)
+            def _(cp=cp):
+                cp.start()
+
+    t_copy.wait_recv()
+    ex, ey = lax.div(e, 4), lax.rem(e, 4)
+    for i in range(4):
+        @pl.when(c >= 4)
+        def _(i=i):
             update(i, slot3, S3)
 
-    t_copy.wait_recv()
-    for i in range(4):
         for t in range(4):
             row, col = 128 * (t // 2), 128 * (t % 2)
             TB[4 * i + t, :, 0:128] = Q[i, row:row + 128, col:col + 128]
             TB[4 * i + t, :, 128:256] = Q[i, row:row + 128, col + 256:col + 384]
-    for i in range(4):
         for j in range(2):
             tile = TB[4 * i + tl[i // 2, i % 2, j]]
             for r in range(4):
                 SB[8 * i + 4 * j + r] = tile[32 * r:32 * r + 32]
-
-    mine = pltpu.make_async_copy(SB.at[2 * e + q], AB.at[q, e], rx)
-    mine.start()
-    remote(SB.at[2 * e + 1 - q], AB.at[q, e], sx, rx, e, peer).start()
-    for k in range(1, 16):
-        o = lax.rem(e + k, 16)
-        for z in range(2):
-            remote(SB.at[2 * o + z], AB.at[q, e], sx, rx, o, 2 * c + z).start()
+        for w in range(4):
+            owner = 4 * w + (w + i) % 4
+            here = e == owner
+            for z in range(2):
+                piece = SB.at[8 * i + 2 * w + z]
+
+                @pl.when(jnp.logical_not(here))
+                def _(piece=piece, owner=owner, z=z):
+                    remote(piece, AB.at[q, e], sx, rx, owner, 2 * c + z).start()
+
+            @pl.when(here)
+            def _(i=i, w=w):
+                pltpu.make_async_copy(SB.at[8 * i + 2 * w + q], AB.at[q, e], rx).start()
+                remote(SB.at[8 * i + 2 * w + 1 - q], AB.at[q, e], sx, rx, e, peer).start()
+
     GF[0:8] = jnp.zeros((8, 32, 256), F32)
     GF[24:32] = jnp.zeros((8, 32, 256), F32)
     pltpu.make_async_copy(AB, AB, rx).wait()
@@ -252,8 +346,7 @@
 
     lax.fori_loop(0, 16, one, 0)
 
-    u, h = lax.div(e, 2), lax.rem(e, 2)
-    blk, j = lax.div(u, 2), lax.rem(u, 2)
+    blk, j, h = lax.rem(ey - ex + 4, 4), lax.div(ex, 2), lax.rem(ex, 2)
     home = lax.div(blk, 2)
     dst = out.at[0, lax.rem(blk, 2), j, pl.ds(pl.multiple_of(h * 64 + q * 32, 32), 32), :]
     is_home = home == q
@@ -293,19 +386,41 @@
 
     @pl.when(c == 5)
     def _():
-        a2a.wait_send()
         a2b.wait_send()
-        s3c.wait_send()
-        s3d.wait_send()
 
     @pl.when(c >= 6)
     def _():
         a2f.wait_send()
 
-    @pl.when(c == 3)
-    def _():
-        s3a.wait_send()
-        s3b.wait_send()
+    @pl.when(c == 6)
+    def _():
+        a2r.wait_send()
+        for cp in s2r:
+            cp.wait_send()
+
+    @pl.when(down_sender)
+    def _():
+        ad.wait_send()
+
+    @pl.when(low_greater & (c == 2))
+    def _():
+        ae.wait_send()
+
+    @pl.when(low_greater & (c == 0))
+    def _():
+        for cp in z2:
+            cp.wait_send()
+
+    @pl.when(c == jnp.where(q == 0, 3, 0))
+    def _():
+        for to in x3:
+            for cp in to:
+                cp.wait_send()
+
+    @pl.when(relay)
+    def _():
+        for cp in hop:
+            cp.wait_send()
 
 
 def shards(retarded, coupling, sigma_lesser, sigma_greater, tiles, offsets):
@@ -314,7 +429,7 @@
     anyspace = pl.BlockSpec(memory_space=pltpu.HBM)
     return pl.pallas_call(
         kernel,
-        out_shape=jax.ShapeDtypeStruct((1, 2, 2, 128, 256), BF),
+        out_shape=pltpu.VMEM((1, 2, 2, 128, 256), BF),
         in_specs=[anyspace] * 5 + [pl.BlockSpec(memory_space=pltpu.SMEM)],
         out_specs=pl.BlockSpec(memory_space=pltpu.VMEM),
         scratch_shapes=[
@@ -323,14 +438,15 @@
             pltpu.VMEM((2,) + mat, BF), pltpu.VMEM((4,) + mat, BF),
             pltpu.VMEM(mat, BF), pltpu.VMEM(mat, BF),
             pltpu.VMEM(mat, BF), pltpu.VMEM(mat, BF), pltpu.VMEM(mat, BF),
+            pltpu.VMEM(mat, BF), pltpu.VMEM(mat, BF), pltpu.VMEM(mat, BF), pltpu.VMEM(mat, BF), pltpu.VMEM(mat, BF),
             pltpu.VMEM((16, 128, 256), BF), pltpu.VMEM((32, 32, 256), BF), pltpu.VMEM((2, 16, 32, 256), BF),
             pltpu.VMEM((16, 32, 256), F32), pltpu.VMEM((32, 32, 256), F32), pltpu.VMEM((16, 32, 256), BF),
             pltpu.SMEM((2, 2, 2), jnp.int32),
-            dma((9,)), dma, dma, dma, dma, dma((5,)), dma((4,)), dma((5,)), dma((3,)), dma((2,)), dma((2,)),
-            dma, dma, dma, dma,
+            dma((9,)), dma, dma, dma, dma, dma((5,)), dma((4,)), dma((5,)), dma((3,)), dma((4,)), dma((4,)),
+            dma((2,)), dma((2,)), dma((6,)), dma((2,)), dma, dma, dma, dma,
         ],
         compiler_params=pltpu.CompilerParams(
-            collective_id=0, has_side_effects=True, vmem_limit_bytes=48 << 20),
+            collective_id=0, has_side_effects=True, vmem_limit_bytes=63 << 20),
         name="recursion",
     )(retarded, coupling, sigma_lesser, sigma_greater, tiles, offsets)
 

time: 65.5 us -> 53.5 us (0.82)
  the two profiles are of different devices: /device:TPU:129 before, /device:TPU:229 now
where the time goes in v2:
time: 53.5 us; the launch traced here: 53.4 us
  Pallas kernels  52.7 us (99%)
  local copies, waits for them, and re-layouts  0.71 us (1%)
    pallas_call x1, Pallas kernels, shards(): pl.pallas_call(kernel, out_shape=pltpu.VMEM((1, 2, 2, 128, 256), BF), in_...  52.7 us

profile of v2, /device:TPU:229, one launch (start us, length us, event | category | flops | bytes accessed | tf_op | source)
XLA Modules:
  0.0 53.4 jit_solution(10727282667933490911)
XLA Ops:
  0.0 52.7 %recursion.1 = bf16[1,2,2,128,256]{4,3,2,1,0:T(8,128)(2,1)S(1)} custom-call(bf16[1,2,256,512]{3,2,1,0:T(8,128)(2,1)} %ret.1, bf16[2,256,512]{2,1,0:T(8,128)(2,1)} %cpl.1, bf16[1,2,256,512]{3,2,1,0:T(8,128)(2,1)} %sl.1, bf16[1,2,256,512]{3,2,1,0:T(8,128)(2,1)} %sg.1, s32[2,2]{1,0:T(2,128)} %tiles_hbm.1, s32[16]{0:T(128)} %offs.1), custom_call_target="tpu_custom_call" | custom-call | tf_op jit(solution)/shard_map/recursion/pallas_call | solution.py:430
  52.7 0.7 %copy.8 = bf16[1,2,2,128,256]{4,3,2,1,0:T(8,128)(2,1)} copy(bf16[1,2,2,128,256]{4,3,2,1,0:T(8,128)(2,1)S(1)} %recursion.1) | data formatting | bytes 524288

commit v3 on v2

--- a/solution.py
+++ b/solution.py
@@ -30,7 +30,7 @@
 
 def kernel(ret, cpl, sl, sg, tiles_hbm, offs, out,
            R, C, SG, PP, T, J, JX, Q, A1, A2, S1, S2, S3, AD, SD, SE, ZB, X3, TB, SB, AB, LF, GF, OB, tl,
-           ld, sp, rp, sj, rj, sa, ra, ss, rs, sd, rd, st, rt, sx3, rx3, sx, rx, so, ro):
+           ld, sp, rp, sj, rj, sa, ra, ss, rs, sd, rd, st, rt, sx3, rx3, sx, rx, so, ro, go):
     e = lax.axis_index("energy")
     d = lax.axis_index("domain")
     c, q = lax.div(d, 2), lax.rem(d, 2)
@@ -54,18 +54,31 @@
     own_tiles.start()
 
     bar = pltpu.get_barrier_semaphore()
-    for k in range(1, 8):
-        pl.semaphore_signal(bar, 1, device_id=(e, at_chip(lax.rem(c + k, 8))), device_id_type=MESH)
+    low = c < 4
+    base4 = 4 * lax.div(c, 4)
+    source = jnp.where(q == 0, 3, 0)
+    for k in range(1, 4):
+        pl.semaphore_signal(bar, 1, device_id=(e, at_chip(base4 + lax.rem(c + k, 4))), device_id_type=MESH)
     pl.semaphore_signal(bar, 1, device_id=(e, peer), device_id_type=MESH)
     for k in range(1, 16):
         for z in range(2):
             pl.semaphore_signal(bar, 1, device_id=(lax.rem(e + k, 16), 2 * c + z), device_id_type=MESH)
 
+    @pl.when(c == source)
+    def _():
+        for k in range(4, 8):
+            pl.semaphore_signal(bar, 1, device_id=(e, at_chip(k)), device_id_type=MESH)
+
     for b in range(2):
         loads[4 * b].wait()
         loads[4 * b + 1].wait()
         PP[2 * q + b] = mul(R[b], C[b]).astype(BF)
-    pl.semaphore_wait(bar, 7 + 1 + 30)
+    pl.semaphore_wait(bar, jnp.where(low, 34, 35))
+
+    @pl.when(jnp.logical_not(low))
+    def _():
+        pl.semaphore_signal(go, 1, device_id=(e, at_chip(source)), device_id_type=MESH)
+
     p_copy = remote(PP.at[pl.ds(2 * q, 2)], PP.at[pl.ds(2 * q, 2)], sp, rp, e, peer)
     p_copy.start()
     own_tiles.wait()
@@ -82,11 +95,11 @@
         J[2 * q + b] = mul_adj(mul(R[b], SG[q, b]).astype(BF), R[b]).astype(BF)
 
     even = lax.rem(c, 2) == 0
-    rows2 = (pl.ds(0, 128), pl.ds(128, 128))
-    low_greater = (c < 4) & (q == 1)
+    rows2 = [pl.ds(64 * p, 64) for p in range(4)]
+    mirrored = (c < 4) & (q == 1)
     below = at_chip(lax.rem(c + 7, 8))
-    down_sender = low_greater & jnp.logical_not(even)
-    down_taker = low_greater & even
+    down_sender = mirrored & jnp.logical_not(even)
+    down_taker = mirrored & even
     ad = remote(T.at[3], AD, sd.at[0], rd.at[0], e, below)
 
     p_copy.wait_recv()
@@ -117,20 +130,21 @@
     dn = remote(Q.at[3], SD, sd.at[1], rd.at[1], e, below)
     ae = remote(A2, A2, sd.at[2], rd.at[2], e, at_chip(lax.rem(c + 6, 8)))
     ze = remote(ZB, SE, sd.at[3], rd.at[3], e, at_chip(lax.rem(c + 6, 8)))
-    z2 = [remote(ZB.at[r], S2.at[r], ss.at[2 * n + 1 + p], rs.at[1 + p], e, at_chip(lax.rem(c + dist, 8)))
+    z2 = [remote(ZB.at[r], S2.at[r], ss.at[4 * n + 1 + p], rs.at[1 + p], e, at_chip(lax.rem(c + dist, 8)))
           for n, dist in enumerate((3, 2)) for p, r in enumerate(rows2)]
 
     def chip_at(distance):
         return at_chip(lax.rem(c + distance * (1 - 2 * q) + 16, 8))
 
-    x3 = [[remote(X3.at[r], S3.at[r], sx3.at[2 * n + p], rx3.at[p], e, chip_at(dist)) for p, r in enumerate(rows2)]
-          for n, dist in enumerate((3, 2, 1))]
+    x3 = [[remote(X3.at[r], S3.at[r], sx3.at[4 * n + p], rx3.at[p], e, chip_at(dist)) for p, r in enumerate(rows2)]
+          for n, dist in enumerate((3, 1, 2))]
     hop = [remote(S3.at[r], S3.at[r], sx3.at[p], rx3.at[p], e, chip_at(1)) for p, r in enumerate(rows2)]
     relay = c == jnp.where(q == 0, 6, 5)
 
-    @pl.when(even & jnp.logical_not(low_greater))
+    @pl.when(even & jnp.logical_not(mirrored))
     def _():
         s1.start()
+        s1.wait_send()
 
     @pl.when(down_sender)
     def _():
@@ -162,6 +176,7 @@
                 cp.start()
             ze.wait_recv()
             X3[...] = (congruence(A2[...], ZB[...]) + SE[...].astype(F32)).astype(BF)
+            pl.semaphore_wait(go, 4)
             for to in x3:
                 for cp in to:
                     cp.start()
@@ -173,8 +188,7 @@
     a2r = remote(A2.at[half], A2.at[half], sa.at[3], ra.at[2], e, at_chip(lax.rem(c + 1, 8)))
     a2f = remote(A2.at[half], A2.at[half], sa.at[4], ra.at[3], e, peer)
 
-    @pl.when(a1_taker)
-    def _():
+    def composites1():
         a1.wait_recv()
         a1f.start()
         a1f.wait_recv()
@@ -186,14 +200,18 @@
                 def _():
                     a2b.start()
 
+    @pl.when(a1_taker)
+    def _():
+        composites1()
+
     s2_low = (c == 1) & (q == 0)
+    s2_sender = ((c == 1) & (q == 0)) | (c == 5)
     far = at_chip(lax.rem(c + jnp.where(c == 1, 2, 1), 8))
     s2a = [remote(Q.at[3, r], S2.at[r], ss.at[1 + p], rs.at[1 + p], e, far) for p, r in enumerate(rows2)]
-    s2b = [remote(Q.at[3, r], S2.at[r], ss.at[3 + p], rs.at[1 + p], e, at_chip(lax.rem(c + 1, 8)))
+    s2b = [remote(Q.at[3, r], S2.at[r], ss.at[5 + p], rs.at[1 + p], e, at_chip(lax.rem(c + 1, 8)))
            for p, r in enumerate(rows2)]
     s2r = [remote(S2.at[r], S2.at[r], ss.at[1 + p], rs.at[1 + p], e, at_chip(lax.rem(c + 1, 8)))
            for p, r in enumerate(rows2)]
-    s2_sender = s2_low | (c == 5)
 
     @pl.when(jnp.logical_not(even))
     def _():
@@ -228,6 +246,7 @@
     @pl.when(c >= 6)
     def _():
         a2b.wait_recv()
+
         a2f.start()
 
         @pl.when(c == 6)
@@ -235,11 +254,8 @@
             a2r.start()
 
         a2f.wait_recv()
-        a_in = stacked(A2[...])
-        for i in range(4):
-            T[8 + i] = jnp.dot(T[4 * slot2 + i], a_in, preferred_element_type=F32).astype(BF)
-
-    @pl.when(even)
+
+    @pl.when(even & mirrored)
     def _():
         s1.wait_send()
 
@@ -252,24 +268,31 @@
             def _(on=on):
                 on.start()
 
+    @pl.when((c == 2) | (c == 3))
+    def _():
         update(3, slot2, S2)
 
         @pl.when((c == 3) & (q == 0))
         def _():
             X3[...] = Q[3]
-            for to in x3:
+            pl.semaphore_wait(go, 4)
+            for cp in x3[0]:
+                cp.start()
+
+        for i in range(3):
+            update(i, slot2, S2)
+
+        @pl.when((c == 3) & (q == 0))
+        def _():
+            for to in x3[1:]:
                 for cp in to:
                     cp.start()
 
-        for i in range(3):
-            update(i, slot2, S2)
-
     @pl.when(s2_low)
     def _():
         for cp in s2b:
             cp.wait_send()
 
-    slot3 = jnp.where(c >= 6, 2, slot2)
 
     @pl.when(c >= 4)
     def _():
@@ -279,13 +302,21 @@
             @pl.when(relay)
             def _(cp=cp):
                 cp.start()
+
+    @pl.when(c >= 6)
+    def _():
+        SE[...] = (congruence(A2[...], S3[...]) + S2[...].astype(F32)).astype(BF)
+
+    @pl.when((c == 4) | (c == 5))
+    def _():
+        SE[...] = S3[...]
 
     t_copy.wait_recv()
     ex, ey = lax.div(e, 4), lax.rem(e, 4)
     for i in range(4):
         @pl.when(c >= 4)
         def _(i=i):
-            update(i, slot3, S3)
+            update(i, slot2, SE)
 
         for t in range(4):
             row, col = 128 * (t // 2), 128 * (t % 2)
@@ -295,20 +326,24 @@
             tile = TB[4 * i + tl[i // 2, i % 2, j]]
             for r in range(4):
                 SB[8 * i + 4 * j + r] = tile[32 * r:32 * r + 32]
-        for w in range(4):
-            owner = 4 * w + (w + i) % 4
-            here = e == owner
-            for z in range(2):
-                piece = SB.at[8 * i + 2 * w + z]
-
-                @pl.when(jnp.logical_not(here))
-                def _(piece=piece, owner=owner, z=z):
-                    remote(piece, AB.at[q, e], sx, rx, owner, 2 * c + z).start()
-
-            @pl.when(here)
-            def _(i=i, w=w):
-                pltpu.make_async_copy(SB.at[8 * i + 2 * w + q], AB.at[q, e], rx).start()
-                remote(SB.at[8 * i + 2 * w + 1 - q], AB.at[q, e], sx, rx, e, peer).start()
+        here = lax.rem(ex + i, 4) == ey
+        for a in (2, 1, 3, 0):
+            w = lax.rem(ex + a, 4)
+            owner = 4 * w + lax.rem(w + i, 4)
+
+            def send(i=i, w=w, owner=owner):
+                for z in range(2):
+                    remote(SB.at[8 * i + 2 * w + z], AB.at[q, e], sx, rx, owner, 2 * c + z).start()
+
+            if a:
+                send()
+            else:
+                pl.when(jnp.logical_not(here))(send)
+
+                @pl.when(here)
+                def _(i=i, w=w):
+                    pltpu.make_async_copy(SB.at[8 * i + 2 * w + q], AB.at[q, e], rx).start()
+                    remote(SB.at[8 * i + 2 * w + 1 - q], AB.at[q, e], sx, rx, e, peer).start()
 
     GF[0:8] = jnp.zeros((8, 32, 256), F32)
     GF[24:32] = jnp.zeros((8, 32, 256), F32)
@@ -327,7 +362,18 @@
         for k in range(16):
             LF[k, rows, :] = jnp.concatenate([lr[k], li[k]], axis=1)
 
-    def one(m, carry):
+    blk, j, h = lax.rem(ey - ex + 4, 4), lax.div(ex, 2), lax.rem(ex, 2)
+    home = lax.div(blk, 2)
+    dst = out.at[0, lax.rem(blk, 2), j, pl.ds(pl.multiple_of(h * 64 + q * 32, 32), 32), :]
+    is_home = home == q
+
+    def far_first(k):
+        return jnp.where(k == 3, 0, jnp.where(k == 0, 2, 2 * k - 1))
+
+    def one(n, carry):
+        ma = lax.rem(ex + far_first(lax.div(n, 4)), 4)
+        mb = lax.rem(ey + far_first(lax.rem(n, 4)), 4)
+        m = 4 * ma + mb
         base = 8 - offs[m]
         for rr in range(4):
             rows = pl.ds(8 * rr, 8)
@@ -342,15 +388,15 @@
                 acc_i = acc_i + (lr * gi + li * gr)
             OB[m, rows, 0:128] = (acc_r * (1.0 / 16)).astype(BF)
             OB[m, rows, 128:256] = (acc_i * (1.0 / 16)).astype(BF)
+
+        @pl.when(n < 15)
+        def _():
+            remote(OB.at[m], dst, so, ro, m, 2 * c + home).start()
+
         return carry
 
     lax.fori_loop(0, 16, one, 0)
 
-    blk, j, h = lax.rem(ey - ex + 4, 4), lax.div(ex, 2), lax.rem(ex, 2)
-    home = lax.div(blk, 2)
-    dst = out.at[0, lax.rem(blk, 2), j, pl.ds(pl.multiple_of(h * 64 + q * 32, 32), 32), :]
-    is_home = home == q
-
     @pl.when(is_home)
     def _():
         pltpu.make_async_copy(OB.at[e], dst, ro).start()
@@ -359,9 +405,6 @@
     def _():
         remote(OB.at[e], dst, so, ro, e, peer).start()
 
-    for k in range(1, 16):
-        m = lax.rem(e + k, 16)
-        remote(OB.at[m], dst, so, ro, m, 2 * c + home).start()
     pltpu.make_async_copy(out, out, ro).wait()
 
     @pl.when(is_home)
@@ -402,16 +445,16 @@
     def _():
         ad.wait_send()
 
-    @pl.when(low_greater & (c == 2))
+    @pl.when(mirrored & (c == 2))
     def _():
         ae.wait_send()
 
-    @pl.when(low_greater & (c == 0))
+    @pl.when(mirrored & (c == 0))
     def _():
         for cp in z2:
             cp.wait_send()
 
-    @pl.when(c == jnp.where(q == 0, 3, 0))
+    @pl.when(c == source)
     def _():
         for to in x3:
             for cp in to:
@@ -434,7 +477,7 @@
         out_specs=pl.BlockSpec(memory_space=pltpu.VMEM),
         scratch_shapes=[
             pltpu.VMEM((2,) + mat, BF), pltpu.VMEM((2,) + mat, BF), pltpu.VMEM((2, 2) + mat, BF),
-            pltpu.VMEM((4,) + mat, BF), pltpu.VMEM((12,) + mat, BF), pltpu.VMEM((4,) + mat, BF),
+            pltpu.VMEM((4,) + mat, BF), pltpu.VMEM((8,) + mat, BF), pltpu.VMEM((4,) + mat, BF),
             pltpu.VMEM((2,) + mat, BF), pltpu.VMEM((4,) + mat, BF),
             pltpu.VMEM(mat, BF), pltpu.VMEM(mat, BF),
             pltpu.VMEM(mat, BF), pltpu.VMEM(mat, BF), pltpu.VMEM(mat, BF),
@@ -442,8 +485,8 @@
             pltpu.VMEM((16, 128, 256), BF), pltpu.VMEM((32, 32, 256), BF), pltpu.VMEM((2, 16, 32, 256), BF),
             pltpu.VMEM((16, 32, 256), F32), pltpu.VMEM((32, 32, 256), F32), pltpu.VMEM((16, 32, 256), BF),
             pltpu.SMEM((2, 2, 2), jnp.int32),
-            dma((9,)), dma, dma, dma, dma, dma((5,)), dma((4,)), dma((5,)), dma((3,)), dma((4,)), dma((4,)),
-            dma((2,)), dma((2,)), dma((6,)), dma((2,)), dma, dma, dma, dma,
+            dma((9,)), dma, dma, dma, dma, dma((5,)), dma((4,)), dma((9,)), dma((5,)), dma((4,)), dma((4,)),
+            dma((2,)), dma((2,)), dma((12,)), dma((4,)), dma, dma, dma, dma, pltpu.SemaphoreType.REGULAR,
         ],
         compiler_params=pltpu.CompilerParams(
             collective_id=0, has_side_effects=True, vmem_limit_bytes=63 << 20),

time: 53.5 us -> 52.1 us (0.974)
  the two profiles are of different devices: /device:TPU:229 before, /device:TPU:227 now
where the time goes in v3:
time: 52.1 us; the launch traced here: 52 us
  Pallas kernels  51.3 us (98%)
  local copies, waits for them, and re-layouts  0.71 us (1%)
    pallas_call x1, Pallas kernels, shards(): pl.pallas_call(kernel, out_shape=pltpu.VMEM((1, 2, 2, 128, 256), BF), in_...  51.3 us

profile of v3, /device:TPU:227, one launch (start us, length us, event | category | flops | bytes accessed | tf_op | source)
XLA Modules:
  0.0 52.0 jit_solution(8813805579456599627)
XLA Ops:
  0.0 51.3 %recursion.1 = bf16[1,2,2,128,256]{4,3,2,1,0:T(8,128)(2,1)S(1)} custom-call(bf16[1,2,256,512]{3,2,1,0:T(8,128)(2,1)} %ret.1, bf16[2,256,512]{2,1,0:T(8,128)(2,1)} %cpl.1, bf16[1,2,256,512]{3,2,1,0:T(8,128)(2,1)} %sl.1, bf16[1,2,256,512]{3,2,1,0:T(8,128)(2,1)} %sg.1, s32[2,2]{1,0:T(2,128)} %tiles_hbm.1, s32[16]{0:T(128)} %offs.1), custom_call_target="tpu_custom_call" | custom-call | tf_op jit(solution)/shard_map/recursion/pallas_call | solution.py:473
  51.3 0.7 %copy.8 = bf16[1,2,2,128,256]{4,3,2,1,0:T(8,128)(2,1)} copy(bf16[1,2,2,128,256]{4,3,2,1,0:T(8,128)(2,1)S(1)} %recursion.1) | data formatting | bytes 524288

commit v4 on v3

--- a/solution.py
+++ b/solution.py
@@ -137,9 +137,8 @@
         return at_chip(lax.rem(c + distance * (1 - 2 * q) + 16, 8))
 
     x3 = [[remote(X3.at[r], S3.at[r], sx3.at[4 * n + p], rx3.at[p], e, chip_at(dist)) for p, r in enumerate(rows2)]
-          for n, dist in enumerate((3, 1, 2))]
+          for n, dist in enumerate((3, 4, 1, 2))]
     hop = [remote(S3.at[r], S3.at[r], sx3.at[p], rx3.at[p], e, chip_at(1)) for p, r in enumerate(rows2)]
-    relay = c == jnp.where(q == 0, 6, 5)
 
     @pl.when(even & jnp.logical_not(mirrored))
     def _():
@@ -298,10 +297,6 @@
     def _():
         for cp in hop:
             cp.wait_recv()
-
-            @pl.when(relay)
-            def _(cp=cp):
-                cp.start()
 
     @pl.when(c >= 6)
     def _():
@@ -459,11 +454,6 @@
         for to in x3:
             for cp in to:
                 cp.wait_send()
-
-    @pl.when(relay)
-    def _():
-        for cp in hop:
-            cp.wait_send()
 
 
 def shards(retarded, coupling, sigma_lesser, sigma_greater, tiles, offsets):
@@ -486,7 +476,7 @@
             pltpu.VMEM((16, 32, 256), F32), pltpu.VMEM((32, 32, 256), F32), pltpu.VMEM((16, 32, 256), BF),
             pltpu.SMEM((2, 2, 2), jnp.int32),
             dma((9,)), dma, dma, dma, dma, dma((5,)), dma((4,)), dma((9,)), dma((5,)), dma((4,)), dma((4,)),
-            dma((2,)), dma((2,)), dma((12,)), dma((4,)), dma, dma, dma, dma, pltpu.SemaphoreType.REGULAR,
+            dma((2,)), dma((2,)), dma((16,)), dma((4,)), dma, dma, dma, dma, pltpu.SemaphoreType.REGULAR,
         ],
         compiler_params=pltpu.CompilerParams(
             collective_id=0, has_side_effects=True, vmem_limit_bytes=63 << 20),

time: 52.1 us -> 50.7 us (0.973)
  Pallas kernels: 51.3 us -> 49.9 us
    pallas_call x1, Pallas kernels: 51.3 us -> 49.9 us  [shards(): pl.pallas_call(kernel, out_shape=pltpu.VMEM((1, 2, 2, 128, 256), BF), in_...]
where the time goes in v4:
time: 50.7 us; the launch traced here: 50.6 us
  Pallas kernels  49.9 us (98%)
  local copies, waits for them, and re-layouts  0.71 us (1%)
    pallas_call x1, Pallas kernels, shards(): pl.pallas_call(kernel, out_shape=pltpu.VMEM((1, 2, 2, 128, 256), BF), in_...  49.9 us

profile of v4, /device:TPU:227, one launch (start us, length us, event | category | flops | bytes accessed | tf_op | source)
XLA Modules:
  0.0 50.6 jit_solution(7405585954879975183)
XLA Ops:
  0.0 49.9 %recursion.1 = bf16[1,2,2,128,256]{4,3,2,1,0:T(8,128)(2,1)S(1)} custom-call(bf16[1,2,256,512]{3,2,1,0:T(8,128)(2,1)} %ret.1, bf16[2,256,512]{2,1,0:T(8,128)(2,1)} %cpl.1, bf16[1,2,256,512]{3,2,1,0:T(8,128)(2,1)} %sl.1, bf16[1,2,256,512]{3,2,1,0:T(8,128)(2,1)} %sg.1, s32[2,2]{1,0:T(2,128)} %tiles_hbm.1, s32[16]{0:T(128)} %offs.1), custom_call_target="tpu_custom_call" | custom-call | tf_op jit(solution)/shard_map/recursion/pallas_call | solution.py:463
  49.9 0.7 %copy.8 = bf16[1,2,2,128,256]{4,3,2,1,0:T(8,128)(2,1)} copy(bf16[1,2,2,128,256]{4,3,2,1,0:T(8,128)(2,1)S(1)} %recursion.1) | data formatting | bytes 524288

commit v5 on v4

--- a/solution.py
+++ b/solution.py
@@ -137,7 +137,7 @@
         return at_chip(lax.rem(c + distance * (1 - 2 * q) + 16, 8))
 
     x3 = [[remote(X3.at[r], S3.at[r], sx3.at[4 * n + p], rx3.at[p], e, chip_at(dist)) for p, r in enumerate(rows2)]
-          for n, dist in enumerate((3, 4, 1, 2))]
+          for n, dist in enumerate(jnp.where(q == 0, a, b) for a, b in zip((3, 4, 2, 1), (3, 1, 2, 4)))]
     hop = [remote(S3.at[r], S3.at[r], sx3.at[p], rx3.at[p], e, chip_at(1)) for p, r in enumerate(rows2)]
 
     @pl.when(even & jnp.logical_not(mirrored))

time: 50.7 us -> 50.7 us (level)
  no operation moved by 1% of the time
where the time goes in v5:
time: 50.7 us; the launch traced here: 50.6 us
  Pallas kernels  49.9 us (98%)
  local copies, waits for them, and re-layouts  0.71 us (1%)
    pallas_call x1, Pallas kernels, shards(): pl.pallas_call(kernel, out_shape=pltpu.VMEM((1, 2, 2, 128, 256), BF), in_...  49.9 us

profile of v5, /device:TPU:227, one launch (start us, length us, event | category | flops | bytes accessed | tf_op | source)
XLA Modules:
  0.0 50.6 jit_solution(10429174843661326177)
XLA Ops:
  0.0 49.9 %recursion.1 = bf16[1,2,2,128,256]{4,3,2,1,0:T(8,128)(2,1)S(1)} custom-call(bf16[1,2,256,512]{3,2,1,0:T(8,128)(2,1)} %ret.1, bf16[2,256,512]{2,1,0:T(8,128)(2,1)} %cpl.1, bf16[1,2,256,512]{3,2,1,0:T(8,128)(2,1)} %sl.1, bf16[1,2,256,512]{3,2,1,0:T(8,128)(2,1)} %sg.1, s32[2,2]{1,0:T(2,128)} %tiles_hbm.1, s32[16]{0:T(128)} %offs.1), custom_call_target="tpu_custom_call" | custom-call | tf_op jit(solution)/shard_map/recursion/pallas_call | solution.py:463
  49.9 0.7 %copy.8 = bf16[1,2,2,128,256]{4,3,2,1,0:T(8,128)(2,1)} copy(bf16[1,2,2,128,256]{4,3,2,1,0:T(8,128)(2,1)S(1)} %recursion.1) | data formatting | bytes 524288
